TPU v7x, 32 devices: a whole 2x2x4 slice. The times are simulated.
32 devices in a mesh: row: 8 (over z, y), col: 4 (over x, core).
Axes of the slice: x: 2, y: 2, z: 4, core: 2. Of those that a mesh axis runs over, the one named last changes fastest.
Arguments:
- start_block: float32 [64, 16, 128], P(('row', 'col')), may hold values from -6 to 6
- blocks: float32 [8, 4, 58, 128, 128], P('row', 'col'), as said below
- slot_row: int32 [8, 4, 58], P('row', 'col'), may hold values from 0 to 7, as said below
- slot_col: int32 [8, 4, 58], P('row', 'col'), may hold values from 0 to 15, as said below
- counts: int32 [8, 4], P('row', 'col'), may hold values from 34 to 58, as said below
Outputs:
- alphas: float32 [2, 16, 16], replicated
- betas: float32 [2, 16, 16], replicated
- next_block: float32 [64, 16, 128], P(('row', 'col'))
Inputs may be any that keep to these rules, and one draw needn't show every extreme that they name: `blocks`: over all cells the live slots list each nonzero block of a symmetric matrix exactly once: block (J, I) is listed exactly when (I, J) is, holding its transpose. Slots at or past a cell's count hold finite values that are no part of H. `counts`: live slots of a cell come first; in every draw some cell has all 58 slots live. `slot_row`: for live slots, the block row within the cell's row group of 8 block rows. `slot_col`: for live slots, the position within the cell's column group of 16 block columns, as in the first step.
All inputs are finite; a program needn't handle non-finite values.
Results may differ from a plain program's by a relative error of at most 0.0003.
Values sent between devices are 32-bit elements; how exact they have to be, the bound alone decides.
A program may use at most 64 MiB of HBM per device.

v0:
```python
import jax
import jax.numpy as jnp
from jax import lax
from jax.sharding import PartitionSpec as P

ITERS = 2
highest = lax.Precision.HIGHEST


def matmul(left, right):
    return jnp.dot(left, right, precision=highest, preferred_element_type=jnp.float32)


def local_gram(left, right):
    return jnp.einsum(
        "bki,bli->kl", left, right, precision=highest, preferred_element_type=jnp.float32
    )


def on_device(start_block, blocks, slot_row, slot_col, counts):
    matrix_tiles = blocks[0, 0]
    rows_local = slot_row[0, 0]
    cols_local = slot_col[0, 0]
    capacity = matrix_tiles.shape[0]
    active = lax.iota(jnp.int32, capacity) < counts[0, 0]
    piece_rows = start_block.shape[0]
    vec_count = start_block.shape[1]
    orbitals = start_block.shape[2]
    row_total = float(piece_rows * lax.axis_size("row") * lax.axis_size("col") * orbitals)
    identity = jnp.eye(vec_count, dtype=jnp.float32)
    start_mean = lax.psum(local_gram(start_block, start_block), ("row", "col")) / row_total
    factor = jnp.linalg.cholesky(start_mean)
    inverse = jax.scipy.linalg.solve_triangular(factor, identity, lower=True)
    vectors = jnp.einsum(
        "kl,bli->bki", inverse, start_block, precision=highest, preferred_element_type=jnp.float32
    )
    previous = jnp.zeros(vectors.shape, jnp.float32)
    beta_prev = jnp.zeros((vec_count, vec_count), jnp.float32)
    alpha_list = []
    beta_list = []
    for iteration in range(ITERS):
        gathered = lax.all_gather(vectors, "row", axis=0, tiled=True)
        operate_product = jnp.einsum(
            "sij,skj->ski",
            matrix_tiles,
            gathered[cols_local],
            precision=highest,
            preferred_element_type=jnp.float32,
        )
        targets = lax.iota(jnp.int32, lax.axis_size("col") * piece_rows)
        selector = ((rows_local[None, :] == targets[:, None]) & active[None, :]).astype(jnp.float32)
        image_block = lax.psum_scatter(
            jnp.einsum(
                "rs,ski->rki",
                selector,
                operate_product,
                precision=highest,
                preferred_element_type=jnp.float32,
            ),
            "col",
            scatter_dimension=0,
            tiled=True,
        )
        stacked = jnp.concatenate([image_block, vectors, previous], axis=1)
        all_means = lax.psum(local_gram(stacked, stacked), ("row", "col")) / row_total
        yy_mean = all_means[:vec_count, :vec_count]
        vy_mean = all_means[vec_count : 2 * vec_count, :vec_count]
        py_mean = all_means[2 * vec_count :, :vec_count]
        vv_mean = all_means[vec_count : 2 * vec_count, vec_count : 2 * vec_count]
        pv_mean = all_means[2 * vec_count :, vec_count : 2 * vec_count]
        pp_mean = all_means[2 * vec_count :, 2 * vec_count :]
        residual = image_block - jnp.einsum(
            "lk,bli->bki", vy_mean, vectors, precision=highest, preferred_element_type=jnp.float32
        )
        residual = residual - jnp.einsum(
            "kl,bli->bki",
            beta_prev,
            previous,
            precision=highest,
            preferred_element_type=jnp.float32,
        )
        gram_mean = yy_mean - matmul(vy_mean.T, vy_mean) - matmul(vy_mean.T, vy_mean)
        gram_mean = gram_mean + matmul(matmul(vy_mean.T, vv_mean), vy_mean)
        gram_mean = gram_mean - matmul(py_mean.T, beta_prev.T) - matmul(beta_prev, py_mean)
        gram_mean = gram_mean + matmul(matmul(vy_mean.T, pv_mean.T), beta_prev.T)
        gram_mean = gram_mean + matmul(matmul(beta_prev, pv_mean), vy_mean)
        gram_mean = gram_mean + matmul(matmul(beta_prev, pp_mean), beta_prev.T)
        factor = jnp.linalg.cholesky(gram_mean)
        beta_block = factor.T
        inverse = jax.scipy.linalg.solve_triangular(factor, identity, lower=True)
        previous = vectors
        vectors = jnp.einsum(
            "kl,bli->bki", inverse, residual, precision=highest, preferred_element_type=jnp.float32
        )
        beta_prev = beta_block
        alpha_list.append(vy_mean)
        beta_list.append(beta_block)
    return (jnp.stack(alpha_list), jnp.stack(beta_list), vectors)


def solution(mesh):
    placed = (
        P(("row", "col"), None, None),
        P("row", "col", None, None, None),
        P("row", "col", None),
        P("row", "col", None),
        P("row", "col"),
    )
    return jax.shard_map(
        on_device,
        mesh=mesh,
        in_specs=placed,
        out_specs=(P(), P(), P(("row", "col"), None, None)),
        check_vma=False,
    )
```

profile of v0, /device:TPU:0, one launch (start us, length us, event | category | flops | bytes accessed | tf_op | source)
XLA Modules:
  0.0 285.7 jit_solution(17474431526224107313)
XLA Ops:
  7.9 0.7 fusion.84
  8.7 42.0 %psum.21 = f32[16,16]{0,1:T(8,128)S(1)} all-reduce(f32[16,16]{0,1:T(8,128)S(1)} %convolution_bitcast_fusion.12), channel_id=1, replica_groups=mesh['row'=8,'col'=4] {'row','col'}, use_global_device_ids=true, to_apply=%region_0.0 | all-reduce | flops 256 | bytes 2048 | tf_op jit(solution)/shard_map/psum | solution.py:31
  50.8 1.5 cholesky.59
  52.9 0.6 fusion.25
  53.6 1.2 custom-call.7
  55.1 30.6 %all_gather.6 = f32[16,16,128]{2,1,0:T(8,128)S(1)} all-gather(f32[2,16,128]{2,1,0:T(8,128)S(1)} %convolution_bitcast_fusion.8), channel_id=1, replica_groups=mesh['row'=8,'col'=4] {'row'}, dimensions={0}, use_global_device_ids=true | all-gather | bytes 147456 | tf_op jit(solution)/shard_map/all_gather | solution.py:42
  86.4 8.1 %fusion.2 = f32[58,16,128]{2,1,0:T(8,128)S(1)} fusion(f32[58,16,128]{2,1,0:T(8,128)S(1)} %gather_fusion, f32[1,1,58,128,128]{4,3,2,1,0:T(8,128)} %param.9), kind=kOutput, calls=%fused_computation.4 | convolution fusion | flops 182452224 | bytes 4751360 | tf_op jit(solution)/shard_map/sij,skj->ski/dot_general | solution.py:43
  95.6 19.3 %reduce-scatter.3.cloned.1.call-done = f32[2,16,128]{2,1,0:T(8,128)} async-done(((f32[8,16,128]{2,1,0:T(8,128)}), f32[2,16,128]{2,1,0:T(8,128)}) %reduce-scatter.3.cloned.1.call-update) | async-done | bytes 16400 | tf_op jit(solution)/shard_map/reduce_scatter | solution.py:52
  114.9 1.0 convolution_bitcast_fusion.1
  115.9 39.5 %psum.22 = f32[48,48]{0,1:T(8,128)S(1)} all-reduce(f32[48,48]{0,1:T(8,128)S(1)} %convolution_bitcast_fusion.1), channel_id=1, replica_groups=mesh['row'=8,'col'=4] {'row','col'}, use_global_device_ids=true, to_apply=%region_4.0 | all-reduce | flops 2304 | bytes 18432 | tf_op jit(solution)/shard_map/psum | solution.py:65
  156.4 0.9 fusion.7
  158.7 1.5 cholesky.70
  160.8 0.6 fusion.94
  161.5 1.2 custom-call.8
  163.0 30.7 %all_gather.7 = f32[16,16,128]{2,1,0:T(8,128)S(1)} all-gather(f32[2,16,128]{2,1,0:T(8,128)S(1)} %convolution_bitcast_fusion.5), channel_id=1, replica_groups=mesh['row'=8,'col'=4] {'row'}, dimensions={0}, use_global_device_ids=true | all-gather | bytes 147456 | tf_op jit(solution)/shard_map/all_gather | solution.py:42
  194.4 8.1 %fusion = f32[58,16,128]{2,1,0:T(8,128)S(1)} fusion(f32[58,16,128]{2,1,0:T(8,128)S(1)} %gather_fusion.1, f32[1,1,58,128,128]{4,3,2,1,0:T(8,128)} %param.9), kind=kOutput, calls=%fused_computation.2 | convolution fusion | flops 182452224 | bytes 4751360 | tf_op jit(solution)/shard_map/sij,skj->ski/dot_general | solution.py:43
  203.6 20.4 %reduce-scatter.5.cloned.1.call-done = f32[2,16,128]{2,1,0:T(8,128)} async-done(((f32[8,16,128]{2,1,0:T(8,128)}), f32[2,16,128]{2,1,0:T(8,128)}) %reduce-scatter.5.cloned.1.call-update) | async-done | bytes 16400 | tf_op jit(solution)/shard_map/reduce_scatter | solution.py:52
  223.9 1.0 convolution_bitcast_fusion
  224.9 39.5 %psum.23 = f32[48,48]{0,1:T(8,128)S(1)} all-reduce(f32[48,48]{0,1:T(8,128)S(1)} %convolution_bitcast_fusion), channel_id=1, replica_groups=mesh['row'=8,'col'=4] {'row','col'}, use_global_device_ids=true, to_apply=%region_6.9 | all-reduce | flops 2304 | bytes 18432 | tf_op jit(solution)/shard_map/psum | solution.py:65
  264.4 0.8 fusion.44
  265.3 0.9 fusion.26
  266.9 0.9 fusion.5
  267.8 0.8 fusion.4
  268.8 0.9 convolution_subtract_fusion.1
  269.7 0.9 convolution_subtract_fusion
  270.6 0.7 copy.58
  271.2 0.8 convolution_add_fusion.2
  272.3 0.9 convolution_add_fusion
  273.2 1.5 cholesky.81
  276.0 1.2 custom-call.9
  277.5 0.7 copy.59
  278.2 0.7 convolution_bitcast_fusion.2
  (60 shorter events, 10.9 us)
Async XLA Ops:
  7.2 1.4 copy-start
  7.2 87.3 %copy-start.1 = (s32[1,1,58]{2,1,0:T(1,128)S(1)}, s32[1,1,58]{2,1,0:T(1,128)}, u32[]{:S(2)}) copy-start(s32[1,1,58]{2,1,0:T(1,128)} %param.10) | copy-start | bytes 700
  7.2 107.7 %reduce-scatter.3.cloned.1.call-start = ((), (), s32[]{:S(2)}) async-start(), calls=%async_computation.2 | async-start | bytes 81920 | tf_op jit(solution)/shard_map/reduce_scatter | solution.py:52
  95.5 128.4 %reduce-scatter.5.cloned.1.call-start = ((), (), s32[]{:S(2)}) async-start(), calls=%async_computation.3 | async-start | bytes 81920 | tf_op jit(solution)/shard_map/reduce_scatter | solution.py:52
Sparse Core Ops, SparseCore 0:
  95.6 19.2 reduce-scatter.2
  203.6 20.2 reduce-scatter.4
where the time goes:
time: 287 us; the launch traced here: 286 us
  blocking collectives  182 us (63%)
  waiting for transfers between devices  39.7 us (14%)
  matrix products  31.8 us (11%)
  between operations  14.8 us (5%)
  other arithmetic  12.8 us (4%)
  local copies, waits for them, and re-layouts  4.25 us (1%)
    psum x2, blocking collectives, on_device(): lax.psum(local_gram(stacked, stacked), ('row', 'col')) / row_total  79 us
    all_gather x2, blocking collectives, on_device(): gathered = lax.all_gather(vectors, 'row', axis=0, tiled=True)  61.3 us
    psum x1, blocking collectives, on_device(): lax.psum(local_gram(start_block, start_block), ('row', 'col')) / row_total  42 us
    reduce_scatter x2, waiting for transfers between devices, on_device(): lax.psum_scatter(jnp.einsum('rs,ski->rki', selector, operate_product, pre...  39.7 us
    dot_general x2, matrix products, on_device(): jnp.einsum('sij,skj->ski', matrix_tiles, gathered[cols_local], precision=...  16.1 us
    dot_general x22, matrix products, matmul(): jnp.dot(left, right, precision=highest, preferred_element_type=jnp.float32)  8.28 us
  transfers between devices with their start and end apart: 2, of which 2 were waited for; matrix products, arithmetic and copies ran while one was open for 0% of the time, Pallas kernels for 0%

commit v1 on v0

--- a/solution.py
+++ b/solution.py
@@ -39,7 +39,15 @@
     alpha_list = []
     beta_list = []
     for iteration in range(ITERS):
-        gathered = lax.all_gather(vectors, "row", axis=0, tiled=True)
+        outer = lax.axis_size("row")
+        val, row_out = (outer, lax.axis_index("row"))
+        gathered, piece_next = (vectors, 1)
+        while piece_next < val:
+            base_arr = lax.ppermute(gathered, "row", [(it, it ^ piece_next) for it in range(val)])
+            u_next = jnp.concatenate([gathered, base_arr], axis=0)
+            left_arr = jnp.concatenate([base_arr, gathered], axis=0)
+            gathered = jnp.where(row_out & piece_next == 0, u_next, left_arr)
+            piece_next = 2 * piece_next
         operate_product = jnp.einsum(
             "sij,skj->ski",
             matrix_tiles,

time: 287 us -> 254 us (0.89)
  blocking collectives: 182 us -> 121 us
  waiting for transfers between devices: 39.7 us -> 54.2 us
  starting transfers between devices: 0.08 us -> 12.8 us
    all_gather x2 -> x0, blocking collectives: 61.3 us -> none  [on_device(): gathered = lax.all_gather(vectors, 'row', axis=0, tiled=True)]
    ppermute x0 -> x6, starting transfers between devices: none -> 12.7 us  [on_device(): lax.ppermute(gathered, 'row', [(it, it ^ piece_next) for it in range(val)])]
    ppermute x0 -> x6, waiting for transfers between devices: none -> 12.3 us  [on_device(): lax.ppermute(gathered, 'row', [(it, it ^ piece_next) for it in range(val)])]
  transfers between devices with their start and end apart: 2 -> 8, of which waited for: 2 -> 8; matrix products, arithmetic and copies ran while one was open for 0% -> 0% of each run, Pallas kernels for 0% -> 0%
where the time goes in v1:
time: 254 us; the launch traced here: 253 us
  blocking collectives  121 us (48%)
  waiting for transfers between devices  54.2 us (21%)
  matrix products  31.8 us (13%)
  between operations  14.8 us (6%)
  starting transfers between devices  12.8 us (5%)
  other arithmetic  12.8 us (5%)
  local copies, waits for them, and re-layouts  4.91 us (2%)
    psum x2, blocking collectives, on_device(): lax.psum(local_gram(stacked, stacked), ('row', 'col')) / row_total  79.2 us
    psum x1, blocking collectives, on_device(): lax.psum(local_gram(start_block, start_block), ('row', 'col')) / row_total  42 us
    reduce_scatter x2, waiting for transfers between devices, on_device(): lax.psum_scatter(jnp.einsum('rs,ski->rki', selector, operate_product, pre...  41.9 us
    dot_general x2, matrix products, on_device(): jnp.einsum('sij,skj->ski', matrix_tiles, gathered[cols_local], precision=...  16.1 us
    ppermute x6, starting transfers between devices, on_device(): lax.ppermute(gathered, 'row', [(it, it ^ piece_next) for it in range(val)])  12.7 us
    ppermute x6, waiting for transfers between devices, on_device(): lax.ppermute(gathered, 'row', [(it, it ^ piece_next) for it in range(val)])  12.3 us
    dot_general x22, matrix products, matmul(): jnp.dot(left, right, precision=highest, preferred_element_type=jnp.float32)  8.28 us
  transfers between devices with their start and end apart: 8, of which 8 were waited for; matrix products, arithmetic and copies ran while one was open for 0% of the time, Pallas kernels for 0%

profile of v1, /device:TPU:0, one launch (start us, length us, event | category | flops | bytes accessed | tf_op | source)
XLA Modules:
  0.0 252.6 jit_solution(13639942345890395916)
XLA Ops:
  8.0 42.0 %psum.21 = f32[16,16]{0,1:T(8,128)S(1)} all-reduce(f32[16,16]{0,1:T(8,128)S(1)} %convolution_bitcast_fusion.12), channel_id=1, replica_groups=mesh['row'=8,'col'=4] {'row','col'}, use_global_device_ids=true, to_apply=%region_0.0 | all-reduce | flops 256 | bytes 2048 | tf_op jit(solution)/shard_map/psum | solution.py:31
  50.1 1.5 cholesky.59
  52.9 1.2 custom-call.7
  54.5 2.3 collective-permute-start
  57.4 1.1 collective-permute-done
  58.5 1.5 collective-permute-start.1
  60.7 1.8 collective-permute-done.1
  62.4 2.6 %collective-permute-start.2 = (f32[8,16,128]{2,1,0:T(8,128)S(1)}, f32[8,16,128]{2,1,0:T(8,128)S(1)}, u32[]{:S(2)}, u32[]{:S(2)}) collective-permute-start(f32[8,16,128]{2,1,0:T(8,128)S(1)} %maximum_select_fusion.2), channel_id=1, source_target_pairs={{0,16},{4,20},{8,24},{12,28},{16,0},{20,4},{24,8},{28,12},{1,17},{... | collective-permute-start | bytes 196616 | tf_op jit(solution)/shard_map/ppermute | solution.py:46
  65.1 2.6 %collective-permute-done.2 = f32[8,16,128]{2,1,0:T(8,128)S(1)} collective-permute-done((f32[8,16,128]{2,1,0:T(8,128)S(1)}, f32[8,16,128]{2,1,0:T(8,128)S(1)}, u32[]{:S(2)}, u32[]{:S(2)}) %collective-permute-start.2) | collective-permute-done | bytes 65568 | tf_op jit(solution)/shard_map/ppermute | solution.py:46
  68.3 8.1 %fusion.2 = f32[58,16,128]{2,1,0:T(8,128)S(1)} fusion(f32[58,16,128]{2,1,0:T(8,128)S(1)} %gather_fusion, f32[1,1,58,128,128]{4,3,2,1,0:T(8,128)} %param.9), kind=kOutput, calls=%fused_computation.4 | convolution fusion | flops 182452224 | bytes 4751360 | tf_op jit(solution)/shard_map/sij,skj->ski/dot_general | solution.py:51
  77.5 20.5 %reduce-scatter.3.cloned.1.call-done = f32[2,16,128]{2,1,0:T(8,128)} async-done(((f32[8,16,128]{2,1,0:T(8,128)}), f32[2,16,128]{2,1,0:T(8,128)}) %reduce-scatter.3.cloned.1.call-update) | async-done | bytes 16400 | tf_op jit(solution)/shard_map/reduce_scatter | solution.py:60
  98.0 1.0 convolution_bitcast_fusion.1
  98.9 39.7 %psum.22 = f32[48,48]{0,1:T(8,128)S(1)} all-reduce(f32[48,48]{0,1:T(8,128)S(1)} %convolution_bitcast_fusion.1), channel_id=1, replica_groups=mesh['row'=8,'col'=4] {'row','col'}, use_global_device_ids=true, to_apply=%region_4.7 | all-reduce | flops 2304 | bytes 18432 | tf_op jit(solution)/shard_map/psum | solution.py:73
  139.7 0.9 fusion.7
  141.9 1.5 cholesky.70
  144.7 1.2 custom-call.8
  146.3 2.3 collective-permute-start.3
  148.6 1.7 collective-permute-done.3
  150.4 1.5 collective-permute-start.4
  151.8 2.5 collective-permute-done.4
  154.3 2.5 collective-permute-start.5
  156.8 2.8 %collective-permute-done.5 = f32[8,16,128]{2,1,0:T(8,128)S(1)} collective-permute-done((f32[8,16,128]{2,1,0:T(8,128)S(1)}, f32[8,16,128]{2,1,0:T(8,128)S(1)}, u32[]{:S(2)}, u32[]{:S(2)}) %collective-permute-start.5) | collective-permute-done | bytes 65568 | tf_op jit(solution)/shard_map/ppermute | solution.py:46
  160.2 8.1 %fusion = f32[58,16,128]{2,1,0:T(8,128)S(1)} fusion(f32[58,16,128]{2,1,0:T(8,128)S(1)} %gather_fusion.1, f32[1,1,58,128,128]{4,3,2,1,0:T(8,128)} %param.9), kind=kOutput, calls=%fused_computation.2 | convolution fusion | flops 182452224 | bytes 4751360 | tf_op jit(solution)/shard_map/sij,skj->ski/dot_general | solution.py:51
  169.4 21.4 %reduce-scatter.5.cloned.1.call-done = f32[2,16,128]{2,1,0:T(8,128)} async-done(((f32[8,16,128]{2,1,0:T(8,128)}), f32[2,16,128]{2,1,0:T(8,128)}) %reduce-scatter.5.cloned.1.call-update) | async-done | bytes 16400 | tf_op jit(solution)/shard_map/reduce_scatter | solution.py:60
  190.8 1.0 convolution_bitcast_fusion
  191.8 39.5 %psum.23 = f32[48,48]{0,1:T(8,128)S(1)} all-reduce(f32[48,48]{0,1:T(8,128)S(1)} %convolution_bitcast_fusion), channel_id=1, replica_groups=mesh['row'=8,'col'=4] {'row','col'}, use_global_device_ids=true, to_apply=%region_6.9 | all-reduce | flops 2304 | bytes 18432 | tf_op jit(solution)/shard_map/psum | solution.py:73
  232.1 0.9 fusion.26
  233.7 0.9 fusion.5
  235.7 0.9 convolution_subtract_fusion.1
  239.1 0.9 convolution_add_fusion
  240.1 1.5 cholesky.81
  242.9 1.2 custom-call.9
  (76 shorter events, 19.0 us)
Async XLA Ops:
  7.2 0.7 copy-start
  7.2 69.2 %copy-start.1 = (s32[1,1,58]{2,1,0:T(1,128)S(1)}, s32[1,1,58]{2,1,0:T(1,128)}, u32[]{:S(2)}) copy-start(s32[1,1,58]{2,1,0:T(1,128)} %param.10) | copy-start | bytes 700
  7.2 90.8 %reduce-scatter.3.cloned.1.call-start = ((), (), s32[]{:S(2)}) async-start(), calls=%async_computation.2 | async-start | bytes 81920 | tf_op jit(solution)/shard_map/reduce_scatter | solution.py:60
  54.5 4.0 %collective-permute-start = (f32[2,16,128]{2,1,0:T(8,128)S(1)}, f32[2,16,128]{2,1,0:T(8,128)S(1)}, u32[]{:S(2)}, u32[]{:S(2)}) collective-permute-start(f32[2,16,128]{2,1,0:T(8,128)S(1)} %convolution_bitcast_fusion.8), channel_id=1, source_target_pairs={{0,4},{4,0},{8,12},{12,8},{16,20},{20,16},{24,28},{28,24},{1,5},{5... | collective-permute-start | bytes 49160 | tf_op jit(solution)/shard_map/ppermute | solution.py:46
  58.5 3.9 %collective-permute-start.1 = (f32[4,16,128]{2,1,0:T(8,128)S(1)}, f32[4,16,128]{2,1,0:T(8,128)S(1)}, u32[]{:S(2)}, u32[]{:S(2)}) collective-permute-start(f32[4,16,128]{2,1,0:T(8,128)S(1)} %maximum_select_fusion.4), channel_id=1, source_target_pairs={{0,8},{4,12},{8,0},{12,4},{16,24},{20,28},{24,16},{28,20},{1,9},{5... | collective-permute-start | bytes 98312 | tf_op jit(solution)/shard_map/ppermute | solution.py:46
  62.4 5.2 %collective-permute-start.2 = (f32[8,16,128]{2,1,0:T(8,128)S(1)}, f32[8,16,128]{2,1,0:T(8,128)S(1)}, u32[]{:S(2)}, u32[]{:S(2)}) collective-permute-start(f32[8,16,128]{2,1,0:T(8,128)S(1)} %maximum_select_fusion.2), channel_id=1, source_target_pairs={{0,16},{4,20},{8,24},{12,28},{16,0},{20,4},{24,8},{28,12},{1,17},{... | collective-permute-start | bytes 196616 | tf_op jit(solution)/shard_map/ppermute | solution.py:46
  77.4 113.3 %reduce-scatter.5.cloned.1.call-start = ((), (), s32[]{:S(2)}) async-start(), calls=%async_computation.3 | async-start | bytes 81920 | tf_op jit(solution)/shard_map/reduce_scatter | solution.py:60
  146.3 4.1 %collective-permute-start.3 = (f32[2,16,128]{2,1,0:T(8,128)S(1)}, f32[2,16,128]{2,1,0:T(8,128)S(1)}, u32[]{:S(2)}, u32[]{:S(2)}) collective-permute-start(f32[2,16,128]{2,1,0:T(8,128)S(1)} %convolution_bitcast_fusion.5), channel_id=1, source_target_pairs={{0,4},{4,0},{8,12},{12,8},{16,20},{20,16},{24,28},{28,24},{1,5},{5... | collective-permute-start | bytes 49160 | tf_op jit(solution)/shard_map/ppermute | solution.py:46
  150.4 3.9 %collective-permute-start.4 = (f32[4,16,128]{2,1,0:T(8,128)S(1)}, f32[4,16,128]{2,1,0:T(8,128)S(1)}, u32[]{:S(2)}, u32[]{:S(2)}) collective-permute-start(f32[4,16,128]{2,1,0:T(8,128)S(1)} %maximum_select_fusion.5), channel_id=1, source_target_pairs={{0,8},{4,12},{8,0},{12,4},{16,24},{20,28},{24,16},{28,20},{1,9},{5... | collective-permute-start | bytes 98312 | tf_op jit(solution)/shard_map/ppermute | solution.py:46
  154.3 5.2 %collective-permute-start.5 = (f32[8,16,128]{2,1,0:T(8,128)S(1)}, f32[8,16,128]{2,1,0:T(8,128)S(1)}, u32[]{:S(2)}, u32[]{:S(2)}) collective-permute-start(f32[8,16,128]{2,1,0:T(8,128)S(1)} %maximum_select_fusion.3), channel_id=1, source_target_pairs={{0,16},{4,20},{8,24},{12,28},{16,0},{20,4},{24,8},{28,12},{1,17},{... | collective-permute-start | bytes 196616 | tf_op jit(solution)/shard_map/ppermute | solution.py:46
Sparse Core Ops, SparseCore 0:
  77.6 20.3 reduce-scatter.2
  169.4 21.3 reduce-scatter.4
